TPU v7x, 128 devices: a whole 4x4x4 slice. The times are simulated.
128 devices in a mesh: row: 16 (over z_hi, y, core), col: 8 (over x, z_lo).
Axes of the slice: x: 4, y: 4, z: 4 (z_hi: 2, z_lo: 2; z = z_hi * 2 + z_lo), core: 2. Of those that a mesh axis runs over, the one named last changes fastest.
Arguments:
- word_topic: bfloat16 [131072, 128], P(('row', 'col')), may hold values from 0.25 to 4
- topic_weight: float32 [128], replicated, may hold values from 0.1 to 10
- tile_blocks: int32 [16, 8, 64, 2], P('row', 'col'), may hold values from 0 to 63, as said below
- tile_live: int32 [16, 8], P('row', 'col'), may hold values from 16 to 64, as said below
- pair_counts: int32 [16, 8, 64, 256, 256], P('row', 'col'), may hold values from 0 to 63
Outputs:
- next_word_topic: bfloat16 [131072, 128], P(('row', 'col'))
- next_topic_weight: float32 [128], replicated
Inputs may be any that keep to these rules, and one draw needn't show every extreme that they name: `tile_blocks`: each entry pair is (a word block among the device's 32 blocks of first words, a word block among its 64 blocks of second words); the slots of one device name distinct tiles. `tile_live`: slots at or beyond a device's count hold no tile; some device fills all slots.
All inputs are finite; a program needn't handle non-finite values.
Results may differ from a plain program's by a relative error of at most 0.0049.
Values may be sent and summed in bfloat16 or wider, within the bound.
No kernel may reach another device: no remote copies, remote signals or barrier semaphores. Data moves between devices by JAX's collectives and lax.ppermute only.
A program may use at most 128 MiB of HBM per device.

v0:
```python
from functools import partial
import jax
import jax.numpy as jnp
from jax import lax
from jax.sharding import PartitionSpec as P

V = 131072
K = 128
BLK = 256
ITERS = 2


def group_step(
    left_blocks, right_blocks, blocks, tiles_all, live, want_row, want_col, group, carry
):
    tile_group = 8
    start = group * tile_group
    row_ids = lax.dynamic_slice_in_dim(blocks[:, 0], start, tile_group)
    col_ids = lax.dynamic_slice_in_dim(blocks[:, 1], start, tile_group)
    tiles = lax.dynamic_slice_in_dim(tiles_all, start, tile_group, 0)
    alive = start + jnp.arange(tile_group, dtype=jnp.int32) < live
    left = left_blocks[row_ids]
    right = right_blocks[col_ids]
    denoms = jnp.einsum("gak,gbk->gab", left, right, preferred_element_type=jnp.float32)
    ratio = jnp.where(alive[:, None, None], tiles.astype(jnp.float32) / denoms, 0.0).astype(
        jnp.bfloat16
    )
    results = []
    place = 0
    row_part = jnp.einsum("gab,gbk->gak", ratio, right, preferred_element_type=jnp.float32)
    results.append(carry[place].at[row_ids].add(row_part))
    place = place + 1
    col_part = jnp.einsum("gab,gak->gbk", ratio, left, preferred_element_type=jnp.float32)
    results.append(carry[place].at[col_ids].add(col_part))
    return tuple(results)


def sweep(left_blocks, right_blocks, blocks, tiles_all, live):
    starts = []
    starts.append(jnp.zeros(left_blocks.shape, jnp.float32))
    starts.append(jnp.zeros(right_blocks.shape, jnp.float32))
    stepper = partial(group_step, left_blocks, right_blocks, blocks, tiles_all, live, True, True)
    turns = (live + 7) // 8
    return lax.fori_loop(0, turns, stepper, tuple(starts))


def local(word_topic, topic_weight, tile_blocks, tile_live, pair_counts):
    blocks = tile_blocks[0, 0]
    live = tile_live[0, 0]
    tiles_all = pair_counts[0, 0]
    weights = word_topic
    shares = topic_weight
    for step in range(ITERS):
        row_phi = lax.all_gather(weights, "col", axis=0, tiled=True)
        col_phi = lax.all_gather(weights, "row", axis=0, tiled=True)
        scaled = (row_phi.astype(jnp.float32) * shares).astype(jnp.bfloat16)
        left_blocks = scaled.reshape(-1, BLK, K)
        right_blocks = col_phi.reshape(-1, BLK, K)
        row_acc, col_acc = sweep(left_blocks, right_blocks, blocks, tiles_all, live)
        row_terms = row_acc.reshape(-1, K)
        col_terms = col_acc.reshape(-1, K)
        row_sum = lax.psum_scatter(row_terms, "col", scatter_dimension=0, tiled=True)
        col_sum = lax.psum_scatter(col_terms, "row", scatter_dimension=0, tiled=True)
        expected = weights.astype(jnp.float32) * (shares * row_sum + col_sum)
        totals = lax.psum(jnp.sum(expected, axis=0), ("row", "col"))
        weights = (V * expected / totals).astype(jnp.bfloat16)
        shares = K * totals / jnp.sum(totals)
    return (weights, shares)


def solution(mesh):
    in_specs = (
        P(("row", "col"), None),
        P(),
        P("row", "col", None, None),
        P("row", "col"),
        P("row", "col", None, None, None),
    )
    out_specs = (P(("row", "col"), None), P())
    return jax.shard_map(local, mesh=mesh, in_specs=in_specs, out_specs=out_specs, check_vma=False)
```

profile of v0, /device:TPU:1, one launch (start us, length us, event | category | flops | bytes accessed | tf_op | source)
XLA Modules:
  0.0 1029.4 jit_solution(16607636807630387287)
XLA Ops:
  9.4 52.8 %all-gather.5.cloned.1.call-done = bf16[8192,128]{1,0:T(8,128)(2,1)} async-done(((bf16[1024,128]{1,0:T(8,128)(2,1)}), bf16[8192,128]{1,0:T(8,128)(2,1)}) %all-gather.5.cloned.1.call-update) | async-done | bytes 2097168 | tf_op jit(solution)/shard_map/all_gather | solution.py:54
  62.1 3.3 multiply_convert_fusion.1
  65.5 57.8 %all-gather.7.cloned.1.call-done = bf16[16384,128]{1,0:T(8,128)(2,1)} async-done(((bf16[1024,128]{1,0:T(8,128)(2,1)}), bf16[16384,128]{1,0:T(8,128)(2,1)}) %all-gather.7.cloned.1.call-update) | async-done | bytes 4194320 | tf_op jit(solution)/shard_map/all_gather | solution.py:55
  123.3 4.2 broadcast.60.clone
  130.0 108.6 %while.24 = (s32[]{:T(128)}, f32[32,256,128]{2,1,0:T(8,128)}, f32[64,256,128]{2,1,0:T(8,128)}, s32[]{:T(128)}, s32[64,2]{0,1:T(2,128)S(1)}, /*index=5*/s32[]{:T(...) while((s32[]{:T(128)}, f32[32,256,128]{2,1,0:T(8,128)}, ...), condition=%wide.region_3.4_spmd, body=%wide.region_0.3_spmd.sunk | while | flops 405276736 | bytes 17835532 | solution.py:44
  138.4 3.4 scatter_fusion.1
  142.3 3.3 scatter_fusion
  154.1 3.3 scatter_fusion.1
  173.3 3.3 scatter_fusion
  185.0 3.4 scatter_fusion.1
  216.0 3.4 scatter_fusion.1
  231.5 3.4 scatter_fusion.1
  235.3 3.4 scatter_fusion
  239.3 103.5 %reduce-scatter.5.cloned.1.call-done = f32[1024,128]{1,0:T(8,128)} async-done(((f32[8192,128]{1,0:T(8,128)}), f32[1024,128]{1,0:T(8,128)}) %reduce-scatter.5.cloned.1.call-update) | async-done | bytes 524304 | tf_op jit(solution)/shard_map/reduce_scatter | solution.py:62
  342.8 106.7 %reduce-scatter.7.cloned.1.call-done = f32[1024,128]{1,0:T(8,128)} async-done(((f32[16384,128]{1,0:T(8,128)}), f32[1024,128]{1,0:T(8,128)}) %reduce-scatter.7.cloned.1.call-update) | async-done | bytes 524304 | tf_op jit(solution)/shard_map/reduce_scatter | solution.py:63
  450.9 65.3 %psum.14 = f32[128]{0:T(128)S(1)} all-reduce(f32[128]{0:T(128)S(1)} %fusion.4), channel_id=1, replica_groups=mesh['row'=16,'col'=8] {'row','col'}, use_global_device_ids=true, to_apply=%region_7.8 | all-reduce | flops 128 | bytes 1024 | tf_op jit(solution)/shard_map/psum | solution.py:65
  520.1 43.9 %all-gather.9.cloned.1.call-done = bf16[8192,128]{1,0:T(8,128)(2,1)} async-done(((bf16[1024,128]{1,0:T(8,128)(2,1)}), bf16[8192,128]{1,0:T(8,128)(2,1)}) %all-gather.9.cloned.1.call-update) | async-done | bytes 2097168 | tf_op jit(solution)/shard_map/all_gather | solution.py:54
  564.1 3.3 multiply_convert_fusion
  567.4 58.3 %all-gather.11.cloned.1.call-done = bf16[16384,128]{1,0:T(8,128)(2,1)} async-done(((bf16[1024,128]{1,0:T(8,128)(2,1)}), bf16[16384,128]{1,0:T(8,128)(2,1)}) %all-gather.11.cloned.1.call-update) | async-done | bytes 4194320 | tf_op jit(solution)/shard_map/all_gather | solution.py:55
  625.7 4.2 broadcast.60
  632.4 108.6 %while.25 = (s32[]{:T(128)}, f32[32,256,128]{2,1,0:T(8,128)}, f32[64,256,128]{2,1,0:T(8,128)}, s32[]{:T(128)}, s32[64,2]{0,1:T(2,128)S(1)}, /*index=5*/s32[]{:T(...) while((s32[]{:T(128)}, f32[32,256,128]{2,1,0:T(8,128)}, ...), condition=%wide.region_12.13_spmd, body=%wide.region_9.12_spmd.sunk | while | flops 405276736 | bytes 17835532 | solution.py:44
  640.8 3.4 scatter_fusion.3
  644.6 3.3 scatter_fusion.2
  656.4 3.3 scatter_fusion.3
  675.6 3.3 scatter_fusion.2
  687.4 3.4 scatter_fusion.3
  718.4 3.4 scatter_fusion.3
  733.9 3.4 scatter_fusion.3
  737.7 3.4 scatter_fusion.2
  741.8 103.4 %reduce-scatter.9.cloned.1.call-done = f32[1024,128]{1,0:T(8,128)} async-done(((f32[8192,128]{1,0:T(8,128)}), f32[1024,128]{1,0:T(8,128)}) %reduce-scatter.9.cloned.1.call-update) | async-done | bytes 524304 | tf_op jit(solution)/shard_map/reduce_scatter | solution.py:62
  845.2 106.7 %reduce-scatter.11.cloned.1.call-done = f32[1024,128]{1,0:T(8,128)} async-done(((f32[16384,128]{1,0:T(8,128)}), f32[1024,128]{1,0:T(8,128)}) %reduce-scatter.11.cloned.1.call-update) | async-done | bytes 524304 | tf_op jit(solution)/shard_map/reduce_scatter | solution.py:63
  953.2 65.5 %psum.15 = f32[128]{0:T(128)S(1)} all-reduce(f32[128]{0:T(128)S(1)} %fusion.5), channel_id=1, replica_groups=mesh['row'=16,'col'=8] {'row','col'}, use_global_device_ids=true, to_apply=%region_16.17 | all-reduce | flops 128 | bytes 1024 | tf_op jit(solution)/shard_map/psum | solution.py:65
  (186 shorter events, 180.9 us)
Async XLA Ops:
  7.2 55.0 %all-gather.5.cloned.1.call-start = ((), (), s32[]{:S(2)}) async-start(), calls=%async_computation.4 | async-start | bytes 2359296 | tf_op jit(solution)/shard_map/all_gather | solution.py:54
  7.9 115.4 %all-gather.7.cloned.1.call-start = ((), (), s32[]{:S(2)}) async-start(), calls=%async_computation.5 | async-start | bytes 4456448 | tf_op jit(solution)/shard_map/all_gather | solution.py:55
  8.6 334.2 %reduce-scatter.5.cloned.1.call-start = ((), (), s32[]{:S(2)}) async-start(), calls=%async_computation.6 | async-start | bytes 4718592 | tf_op jit(solution)/shard_map/reduce_scatter | solution.py:62
  127.6 2.5 copy-start.2
  238.7 210.9 %reduce-scatter.7.cloned.1.call-start = ((), (), s32[]{:S(2)}) async-start(), calls=%async_computation.7 | async-start | bytes 8912896 | tf_op jit(solution)/shard_map/reduce_scatter | solution.py:63
  238.7 210.8 %copy-start.1 = (bf16[1024,128]{1,0:T(8,128)(2,1)S(1)}, bf16[1024,128]{1,0:T(8,128)(2,1)}, u32[]{:S(2)}) copy-start(bf16[1024,128]{1,0:T(8,128)(2,1)} %param.9) | copy-start | bytes 786436
  238.7 210.8 %copy-start.3 = (f32[128]{0:T(128)S(1)}, f32[128]{0:T(128)}, u32[]{:S(2)}) copy-start(f32[128]{0:T(128)} %param.10) | copy-start | bytes 1540
  239.3 324.8 %all-gather.9.cloned.1.call-start = ((), (), s32[]{:S(2)}) async-start(), calls=%async_computation.8 | async-start | bytes 2359296 | tf_op jit(solution)/shard_map/all_gather | solution.py:54
  518.2 107.5 %all-gather.11.cloned.1.call-start = ((), (), s32[]{:S(2)}) async-start(), calls=%async_computation.9 | async-start | bytes 4456448 | tf_op jit(solution)/shard_map/all_gather | solution.py:55
  518.8 326.4 %reduce-scatter.9.cloned.1.call-start = ((), (), s32[]{:S(2)}) async-start(), calls=%async_computation.10 | async-start | bytes 4718592 | tf_op jit(solution)/shard_map/reduce_scatter | solution.py:62
  741.0 210.8 %reduce-scatter.11.cloned.1.call-start = ((), (), s32[]{:S(2)}) async-start(), calls=%async_computation.11 | async-start | bytes 8912896 | tf_op jit(solution)/shard_map/reduce_scatter | solution.py:63
  741.1 210.8 %copy-start = (bf16[1024,128]{1,0:T(8,128)(2,1)S(1)}, bf16[1024,128]{1,0:T(8,128)(2,1)}, u32[]{:S(2)}) copy-start(bf16[1024,128]{1,0:T(8,128)(2,1)} %divide_convert_fusion.1) | copy-start | bytes 786436
Sparse Core Ops, SparseCore 0:
  9.6 52.4 all-gather.4
  64.6 58.7 all-gather.6
  238.8 103.9 reduce-scatter.4
  347.0 102.4 reduce-scatter.6
  518.3 45.6 all-gather.8
  566.9 58.7 all-gather.10
  741.2 103.9 reduce-scatter.8
  849.5 102.2 reduce-scatter.10
where the time goes:
time: 1030 us
  waiting for transfers between devices  636 us (62%)
  blocking collectives  131 us (13%)
  other arithmetic  120 us (12%)
  local copies, waits for them, and re-layouts  84.5 us (8%)
  matrix products  41.8 us (4%)
  between operations  14.8 us (1%)
    reduce_scatter x2, waiting for transfers between devices, local(): lax.psum_scatter(col_terms, 'row', scatter_dimension=0, tiled=True)  213 us
    reduce_scatter x2, waiting for transfers between devices, local(): lax.psum_scatter(row_terms, 'col', scatter_dimension=0, tiled=True)  207 us
    psum x2, blocking collectives, local(): totals = lax.psum(jnp.sum(expected, axis=0), ('row', 'col'))  131 us
    all_gather x2, waiting for transfers between devices, local(): col_phi = lax.all_gather(weights, 'row', axis=0, tiled=True)  116 us
    all_gather x2, waiting for transfers between devices, local(): row_phi = lax.all_gather(weights, 'col', axis=0, tiled=True)  96.7 us
    scatter-add x14, other arithmetic, group_step(): results.append(carry[place].at[col_ids].add(col_part))  46.9 us
    scatter-add x14, other arithmetic, group_step(): results.append(carry[place].at[row_ids].add(row_part))  46.4 us
    gather x14, local copies, waits for them, and re-layouts, group_step(): right = right_blocks[col_ids]  39.7 us
  transfers between devices with their start and end apart: 8, of which 8 were waited for; matrix products, arithmetic and copies ran while one was open for 1% of the time, Pallas kernels for 0%

commit v1 on v0

--- a/solution.py
+++ b/solution.py
@@ -62,7 +62,7 @@
         row_sum = lax.psum_scatter(row_terms, "col", scatter_dimension=0, tiled=True)
         col_sum = lax.psum_scatter(col_terms, "row", scatter_dimension=0, tiled=True)
         expected = weights.astype(jnp.float32) * (shares * row_sum + col_sum)
-        totals = lax.psum(jnp.sum(expected, axis=0), ("row", "col"))
+        totals = lax.psum(lax.psum(jnp.sum(expected, axis=0), "row"), "col")
         weights = (V * expected / totals).astype(jnp.bfloat16)
         shares = K * totals / jnp.sum(totals)
     return (weights, shares)

time: 1030 us -> 1010 us (0.981)
  blocking collectives: 131 us -> 98.6 us
    psum x2 -> x4, blocking collectives: 131 us -> 98.6 us  [local(): totals = lax.psum(lax.psum(jnp.sum(expected, axis=0), 'row'), 'col')]
where the time goes in v1:
time: 1010 us; the launch traced here: 1000 us
  waiting for transfers between devices  640 us (63%)
  other arithmetic  120 us (12%)
  blocking collectives  98.6 us (10%)
  local copies, waits for them, and re-layouts  84.5 us (8%)
  matrix products  41.8 us (4%)
  between operations  14.8 us (1%)
    reduce_scatter x2, waiting for transfers between devices, local(): lax.psum_scatter(col_terms, 'row', scatter_dimension=0, tiled=True)  213 us
    reduce_scatter x2, waiting for transfers between devices, local(): lax.psum_scatter(row_terms, 'col', scatter_dimension=0, tiled=True)  207 us
    all_gather x2, waiting for transfers between devices, local(): col_phi = lax.all_gather(weights, 'row', axis=0, tiled=True)  116 us
    all_gather x2, waiting for transfers between devices, local(): row_phi = lax.all_gather(weights, 'col', axis=0, tiled=True)  101 us
    psum x4, blocking collectives, local(): totals = lax.psum(lax.psum(jnp.sum(expected, axis=0), 'row'), 'col')  98.6 us
    scatter-add x14, other arithmetic, group_step(): results.append(carry[place].at[col_ids].add(col_part))  46.9 us
    scatter-add x14, other arithmetic, group_step(): results.append(carry[place].at[row_ids].add(row_part))  46.4 us
    gather x14, local copies, waits for them, and re-layouts, group_step(): right = right_blocks[col_ids]  39.7 us
  transfers between devices with their start and end apart: 8, of which 8 were waited for; matrix products, arithmetic and copies ran while one was open for 1% of the time, Pallas kernels for 0%

profile of v1, /device:TPU:1, one launch (start us, length us, event | category | flops | bytes accessed | tf_op | source)
XLA Modules:
  0.0 1001.1 jit_solution(5540350984035442466)
XLA Ops:
  9.4 52.8 %all-gather.5.cloned.1.call-done = bf16[8192,128]{1,0:T(8,128)(2,1)} async-done(((bf16[1024,128]{1,0:T(8,128)(2,1)}), bf16[8192,128]{1,0:T(8,128)(2,1)}) %all-gather.5.cloned.1.call-update) | async-done | bytes 2097168 | tf_op jit(solution)/shard_map/all_gather | solution.py:54
  62.1 3.3 multiply_convert_fusion.1
  65.5 57.8 %all-gather.7.cloned.1.call-done = bf16[16384,128]{1,0:T(8,128)(2,1)} async-done(((bf16[1024,128]{1,0:T(8,128)(2,1)}), bf16[16384,128]{1,0:T(8,128)(2,1)}) %all-gather.7.cloned.1.call-update) | async-done | bytes 4194320 | tf_op jit(solution)/shard_map/all_gather | solution.py:55
  123.3 4.2 broadcast.60.clone
  130.0 108.6 %while.24 = (s32[]{:T(128)}, f32[32,256,128]{2,1,0:T(8,128)}, f32[64,256,128]{2,1,0:T(8,128)}, s32[]{:T(128)}, s32[64,2]{0,1:T(2,128)S(1)}, /*index=5*/s32[]{:T(...) while((s32[]{:T(128)}, f32[32,256,128]{2,1,0:T(8,128)}, ...), condition=%wide.region_3.4_spmd, body=%wide.region_0.3_spmd.sunk | while | flops 405276736 | bytes 17835532 | solution.py:44
  138.4 3.4 scatter_fusion.1
  142.3 3.3 scatter_fusion
  173.3 3.3 scatter_fusion
  185.0 3.4 scatter_fusion.1
  216.0 3.4 scatter_fusion.1
  231.5 3.4 scatter_fusion.1
  235.3 3.4 scatter_fusion
  239.3 103.5 %reduce-scatter.5.cloned.1.call-done = f32[1024,128]{1,0:T(8,128)} async-done(((f32[8192,128]{1,0:T(8,128)}), f32[1024,128]{1,0:T(8,128)}) %reduce-scatter.5.cloned.1.call-update) | async-done | bytes 524304 | tf_op jit(solution)/shard_map/reduce_scatter | solution.py:62
  342.8 106.7 %reduce-scatter.7.cloned.1.call-done = f32[1024,128]{1,0:T(8,128)} async-done(((f32[16384,128]{1,0:T(8,128)}), f32[1024,128]{1,0:T(8,128)}) %reduce-scatter.7.cloned.1.call-update) | async-done | bytes 524304 | tf_op jit(solution)/shard_map/reduce_scatter | solution.py:63
  450.9 34.2 %psum.28 = f32[128]{0:T(128)S(1)} all-reduce(f32[128]{0:T(128)S(1)} %fusion.4), channel_id=1, replica_groups=mesh['row'=16,'col'=8] {'row'}, use_global_device_ids=true, to_apply=%region_7.8 | all-reduce | flops 128 | bytes 1024 | tf_op jit(solution)/shard_map/psum | solution.py:65
  485.1 15.0 %psum.29 = f32[128]{0:T(128)S(1)} all-reduce(f32[128]{0:T(128)S(1)} %psum.28), channel_id=1, replica_groups=mesh['row'=16,'col'=8] {'col'}, use_global_device_ids=true, to_apply=%region_8.9 | all-reduce | flops 128 | bytes 1024 | tf_op jit(solution)/shard_map/psum | solution.py:65
  504.1 47.8 %all-gather.9.cloned.1.call-done = bf16[8192,128]{1,0:T(8,128)(2,1)} async-done(((bf16[1024,128]{1,0:T(8,128)(2,1)}), bf16[8192,128]{1,0:T(8,128)(2,1)}) %all-gather.9.cloned.1.call-update) | async-done | bytes 2097168 | tf_op jit(solution)/shard_map/all_gather | solution.py:54
  551.9 3.3 multiply_convert_fusion
  555.2 58.3 %all-gather.11.cloned.1.call-done = bf16[16384,128]{1,0:T(8,128)(2,1)} async-done(((bf16[1024,128]{1,0:T(8,128)(2,1)}), bf16[16384,128]{1,0:T(8,128)(2,1)}) %all-gather.11.cloned.1.call-update) | async-done | bytes 4194320 | tf_op jit(solution)/shard_map/all_gather | solution.py:55
  613.5 4.2 broadcast.60
  620.2 108.6 %while.25 = (s32[]{:T(128)}, f32[32,256,128]{2,1,0:T(8,128)}, f32[64,256,128]{2,1,0:T(8,128)}, s32[]{:T(128)}, s32[64,2]{0,1:T(2,128)S(1)}, /*index=5*/s32[]{:T(...) while((s32[]{:T(128)}, f32[32,256,128]{2,1,0:T(8,128)}, ...), condition=%wide.region_13.14_spmd, body=%wide.region_10.13_spmd.sunk | while | flops 405276736 | bytes 17835532 | solution.py:44
  628.6 3.4 scatter_fusion.3
  632.4 3.3 scatter_fusion.2
  663.4 3.3 scatter_fusion.2
  675.2 3.4 scatter_fusion.3
  706.2 3.4 scatter_fusion.3
  721.7 3.4 scatter_fusion.3
  725.5 3.4 scatter_fusion.2
  729.6 103.4 %reduce-scatter.9.cloned.1.call-done = f32[1024,128]{1,0:T(8,128)} async-done(((f32[8192,128]{1,0:T(8,128)}), f32[1024,128]{1,0:T(8,128)}) %reduce-scatter.9.cloned.1.call-update) | async-done | bytes 524304 | tf_op jit(solution)/shard_map/reduce_scatter | solution.py:62
  833.0 106.7 %reduce-scatter.11.cloned.1.call-done = f32[1024,128]{1,0:T(8,128)} async-done(((f32[16384,128]{1,0:T(8,128)}), f32[1024,128]{1,0:T(8,128)}) %reduce-scatter.11.cloned.1.call-update) | async-done | bytes 524304 | tf_op jit(solution)/shard_map/reduce_scatter | solution.py:63
  941.0 34.5 %psum.30 = f32[128]{0:T(128)S(1)} all-reduce(f32[128]{0:T(128)S(1)} %fusion.5), channel_id=1, replica_groups=mesh['row'=16,'col'=8] {'row'}, use_global_device_ids=true, to_apply=%region_17.18 | all-reduce | flops 128 | bytes 1024 | tf_op jit(solution)/shard_map/psum | solution.py:65
  975.5 14.9 %psum.31 = f32[128]{0:T(128)S(1)} all-reduce(f32[128]{0:T(128)S(1)} %psum.30), channel_id=1, replica_groups=mesh['row'=16,'col'=8] {'col'}, use_global_device_ids=true, to_apply=%region_18.19 | all-reduce | flops 128 | bytes 1024 | tf_op jit(solution)/shard_map/psum | solution.py:65
  (188 shorter events, 187.6 us)
Async XLA Ops:
  7.2 55.0 %all-gather.5.cloned.1.call-start = ((), (), s32[]{:S(2)}) async-start(), calls=%async_computation.4 | async-start | bytes 2359296 | tf_op jit(solution)/shard_map/all_gather | solution.py:54
  7.9 115.4 %all-gather.7.cloned.1.call-start = ((), (), s32[]{:S(2)}) async-start(), calls=%async_computation.5 | async-start | bytes 4456448 | tf_op jit(solution)/shard_map/all_gather | solution.py:55
  8.6 334.2 %reduce-scatter.5.cloned.1.call-start = ((), (), s32[]{:S(2)}) async-start(), calls=%async_computation.6 | async-start | bytes 4718592 | tf_op jit(solution)/shard_map/reduce_scatter | solution.py:62
  127.6 2.5 copy-start.2
  238.7 210.9 %reduce-scatter.7.cloned.1.call-start = ((), (), s32[]{:S(2)}) async-start(), calls=%async_computation.7 | async-start | bytes 8912896 | tf_op jit(solution)/shard_map/reduce_scatter | solution.py:63
  238.7 210.8 %copy-start.1 = (bf16[1024,128]{1,0:T(8,128)(2,1)S(1)}, bf16[1024,128]{1,0:T(8,128)(2,1)}, u32[]{:S(2)}) copy-start(bf16[1024,128]{1,0:T(8,128)(2,1)} %param.9) | copy-start | bytes 786436
  238.7 210.8 %copy-start.3 = (f32[128]{0:T(128)S(1)}, f32[128]{0:T(128)}, u32[]{:S(2)}) copy-start(f32[128]{0:T(128)} %param.10) | copy-start | bytes 1540
  239.3 312.6 %all-gather.9.cloned.1.call-start = ((), (), s32[]{:S(2)}) async-start(), calls=%async_computation.8 | async-start | bytes 2359296 | tf_op jit(solution)/shard_map/all_gather | solution.py:54
  502.1 111.3 %all-gather.11.cloned.1.call-start = ((), (), s32[]{:S(2)}) async-start(), calls=%async_computation.9 | async-start | bytes 4456448 | tf_op jit(solution)/shard_map/all_gather | solution.py:55
  502.7 330.3 %reduce-scatter.9.cloned.1.call-start = ((), (), s32[]{:S(2)}) async-start(), calls=%async_computation.10 | async-start | bytes 4718592 | tf_op jit(solution)/shard_map/reduce_scatter | solution.py:62
  728.8 210.8 %reduce-scatter.11.cloned.1.call-start = ((), (), s32[]{:S(2)}) async-start(), calls=%async_computation.11 | async-start | bytes 8912896 | tf_op jit(solution)/shard_map/reduce_scatter | solution.py:63
  728.9 210.8 %copy-start = (bf16[1024,128]{1,0:T(8,128)(2,1)S(1)}, bf16[1024,128]{1,0:T(8,128)(2,1)}, u32[]{:S(2)}) copy-start(bf16[1024,128]{1,0:T(8,128)(2,1)} %divide_convert_fusion.1) | copy-start | bytes 786436
Sparse Core Ops, SparseCore 0:
  9.6 52.4 all-gather.4
  64.6 58.7 all-gather.6
  238.8 103.9 reduce-scatter.4
  347.0 102.4 reduce-scatter.6
  502.2 49.5 all-gather.8
  554.7 58.7 all-gather.10
  729.0 103.9 reduce-scatter.8
  837.3 102.2 reduce-scatter.10
